TPU v7x, 128 devices: a whole 4x4x4 slice. The times are simulated.
128 devices in a mesh: grp: 4 (over x_hi, core), dev: 32 (over x_lo, z, y).
Axes of the slice: x: 4 (x_hi: 2, x_lo: 2; x = x_hi * 2 + x_lo), y: 4, z: 4, core: 2. Of those that a mesh axis runs over, the one named last changes fastest.
Arguments:
- points: float32 [131072, 128], P(('grp', 'dev')), may hold values from -0.6 to 0.6
- weights: float32 [131072, 128], P(('grp', 'dev')), may hold values from -0.12 to 0.12
- skel_index: int32 [128, 128], P(('grp', 'dev')), may hold values from 0 to 1023
- projection: float32 [128, 128, 1024], P(('grp', 'dev')), may hold values from -0.1875 to 0.1875
- top_index: int32 [4, 256], P('grp'), may hold values from 0 to 4095
- subtree_projection: float32 [4, 256, 4096], P('grp', None, 'dev'), may hold values from -0.09375 to 0.09375
- near_leaf_mask: int32 [128, 3], P(('grp', 'dev')), may hold values from 0 to 1, as said below
Outputs:
- potential: float32 [131072, 128], P(('grp', 'dev'))
Inputs may be any that keep to these rules, and one draw needn't show every extreme that they name: `near_leaf_mask`: entry [l, 1] (the leaf itself) is 1; entries that name a leaf outside the subtree are 0.
All inputs are finite; a program needn't handle non-finite values.
Results may differ from a plain program's by a relative error of at most 0.0003.
Values sent between devices are 32-bit elements; how exact they have to be, the bound alone decides.
No kernel may reach another device: no remote copies, remote signals or barrier semaphores. Data moves between devices by JAX's collectives and lax.ppermute only.
A program may use at most 64 MiB of HBM per device.

v0:
```python
import jax
import jax.numpy as jnp
from jax import lax
from jax.sharding import PartitionSpec as P

PRECISION_HIGH = lax.Precision.HIGHEST


def in_one_piece(arrays, axis, dim, along):
    both = jnp.concatenate(arrays, axis=along)
    result, at, done = (lax.all_gather(both, axis, axis=dim, tiled=True), 0, [])
    for a in arrays:
        done.append(lax.slice_in_dim(result, at, at + a.shape[along], axis=along))
        at += a.shape[along]
    return tuple(done)


def rows_for(lines, size):
    spare = -len(lines) % size
    return jnp.pad(lines, [(0, spare)] + [(0, 0)] * (lines.ndim - 1))


def copy_for_each(shard, axis):
    size = lax.axis_size(axis)
    return lax.all_to_all(
        jnp.broadcast_to(shard[None], (size, *shard.shape)), axis, 0, 0, tiled=True
    )


def in_order(blocks, dim):
    lengths = list(blocks.shape[1:])
    lengths[dim] *= blocks.shape[0]
    return jnp.moveaxis(blocks, 0, dim).reshape(lengths)


def collect(shard, axis, dim):
    blocks = copy_for_each(shard, axis)
    return in_order(blocks, dim)


def split_up(shard, dim, size):
    lengths = shard.shape
    blocks = shard.reshape(*lengths[:dim], size, lengths[dim] // size, *lengths[dim + 1 :])
    return jnp.moveaxis(blocks, dim, 0)


def sent_and_summed(shard, axis, dim):
    blocks = split_up(shard, dim, lax.axis_size(axis))
    arrived = lax.all_to_all(blocks, axis, split_axis=0, concat_axis=0, tiled=True)
    return arrived.sum(axis=0)


def nested_sum(shard, axes):
    padded = rows_for(shard, lax.axis_size(axes))
    whole = collect(sent_and_summed(padded, axes, 0), axes, 0)
    return lax.slice_in_dim(whole, 0, len(shard)).reshape(shard.shape)


def together(arrays, axis):
    ends = [0]
    for a in arrays:
        ends.append(ends[-1] + a.size)
    subtotal = nested_sum(jnp.concatenate([a.ravel() for a in arrays]), axis)
    return tuple((subtotal[b:e].reshape(a.shape) for a, b, e in zip(arrays, ends, ends[1:])))


def extended(cells, sides, width):
    for axis, dim in sides:
        count = lax.axis_size(axis)
        ends = count - 1
        head = lax.slice_in_dim(cells, 0, width, axis=dim)
        tail = lax.slice_in_dim(cells, cells.shape[dim] - width, cells.shape[dim], axis=dim)
        cells = jnp.concatenate(
            [
                lax.ppermute(tail, axis, [(i, (i + 1) % count) for i in range(ends)]),
                cells,
                lax.ppermute(head, axis, [((i + 1) % count, i) for i in range(ends)]),
            ],
            axis=dim,
        )
    return cells


def kernel_tile(left, right):
    left_sq = jnp.sum(left * left, axis=1)
    right_sq = jnp.sum(right * right, axis=1)
    cross = jnp.dot(left, right.T, precision=PRECISION_HIGH, preferred_element_type=jnp.float32)
    return jnp.exp(-0.5 * (left_sq[:, None] + right_sq[None, :] - 2.0 * cross))


def pick_rows(table, index):
    return table[index]


def near_tasks(window, live, target_position, source_slot, out_slot, count, leaf, feats):
    win_pts = window[:, :feats]
    win_wts = window[:, feats:]
    rhs = win_wts.shape[1]

    def step(task, acc):

        def compute(unused):
            target = lax.dynamic_slice_in_dim(win_pts, target_position[task] * leaf, leaf, 0)
            source = lax.dynamic_slice_in_dim(win_pts, source_slot[task] * leaf, leaf, 0)
            source_w = lax.dynamic_slice_in_dim(win_wts, source_slot[task] * leaf, leaf, 0)
            return jnp.dot(
                kernel_tile(target, source),
                source_w,
                precision=PRECISION_HIGH,
                preferred_element_type=jnp.float32,
            )

        def skip(unused):
            return jnp.zeros((leaf, rhs), jnp.float32)

        term = lax.cond(live[task] > 0, compute, skip, 0)
        return lax.dynamic_update_index_in_dim(acc, acc[out_slot[task]] + term, out_slot[task], 0)

    return lax.fori_loop(0, live.shape[0], step, jnp.zeros((count, leaf, rhs), jnp.float32))


def local(points, weights, skel_index, projection, top_index, subtree_projection, near_leaf_mask):
    leaf_dev = near_leaf_mask.shape[0]
    leaf = points.shape[0] // leaf_dev
    feats = points.shape[1]
    rhs = weights.shape[1]
    skel = skel_index.shape[1]
    skeleton_top_level = top_index.shape[1]
    slots = 3 * leaf_dev
    position = lax.axis_index("dev")
    group = lax.axis_index("grp")
    leaf_pts = points.reshape(leaf_dev, leaf, feats)
    leaf_weight_values = weights.reshape(leaf_dev, leaf, rhs)
    skeleton_point_rows = jax.vmap(pick_rows)(leaf_pts, skel_index).reshape(leaf_dev * skel, feats)
    skeleton_weight_values = jnp.einsum(
        "vct,vta->vca", projection, leaf_weight_values, precision=PRECISION_HIGH
    ).reshape(leaf_dev * skel, rhs)
    cands = leaf_dev * skel
    cand_ids = position * cands + jnp.arange(cands, dtype=jnp.int32)
    picker = (top_index[0][:, None] == cand_ids[None, :]).astype(jnp.float32)
    top_pts_part = jnp.dot(
        picker, skeleton_point_rows, precision=PRECISION_HIGH, preferred_element_type=jnp.float32
    )
    top_wts_part = jnp.dot(
        subtree_projection[0],
        skeleton_weight_values,
        precision=PRECISION_HIGH,
        preferred_element_type=jnp.float32,
    )
    near_float = near_leaf_mask.astype(jnp.float32)
    base = (position - 1) * leaf_dev
    slot_ids = jnp.arange(slots, dtype=jnp.int32)
    empty = jnp.zeros((leaf_dev, leaf, rhs), jnp.float32)
    piece_pts, piece_wts = in_one_piece((skeleton_point_rows, skeleton_weight_values), "dev", 0, 1)
    rows = piece_pts.shape[0]
    block_rows = 512

    def block(index, total):
        block_pts = lax.dynamic_slice_in_dim(piece_pts, index * block_rows, block_rows, 0)
        block_wts = lax.dynamic_slice_in_dim(piece_wts, index * block_rows, block_rows, 0)
        leaf_ids = (index * block_rows + jnp.arange(block_rows, dtype=jnp.int32)) // skel
        hits = (leaf_ids[:, None] == base + slot_ids[None, :]).astype(jnp.float32)
        near_col = jnp.sum(near_float[:, None, :] * hits[None, :, :], axis=2)
        tile = kernel_tile(points, block_pts).reshape(leaf_dev, leaf, block_rows)
        far_w = block_wts[None, :, :] * (1.0 - near_col)[:, :, None]
        return total + jnp.einsum("tpb,tbr->tpr", tile, far_w, precision=PRECISION_HIGH)

    far = lax.fori_loop(0, rows // block_rows, block, empty)
    top_pts, top_wts = together((top_pts_part, top_wts_part), "dev")
    top_piece_pts, top_piece_wts = in_one_piece((top_pts, top_wts), "grp", 0, 1)
    rows = top_piece_pts.shape[0]
    owner = jnp.arange(rows, dtype=jnp.int32) // skeleton_top_level
    kept = top_piece_wts * (owner != group).astype(jnp.float32)[:, None]
    top = jnp.dot(
        kernel_tile(points, top_piece_pts),
        kept,
        precision=PRECISION_HIGH,
        preferred_element_type=jnp.float32,
    )
    joined = jnp.concatenate([points, weights], axis=1)
    window = extended(joined, (("dev", 0),), leaf_dev * leaf)
    flat = near_leaf_mask.reshape(-1)
    task = jnp.arange(leaf_dev * slots, dtype=jnp.int32)
    own_target = leaf_dev + task // slots
    own_source = task % slots
    own_out = task // slots
    near = near_tasks(window, flat, own_target, own_source, own_out, leaf_dev, leaf, feats)
    return (near + far).reshape(leaf_dev * leaf, rhs) + top


def solution(mesh):
    return jax.shard_map(
        local,
        mesh=mesh,
        in_specs=(
            P(("grp", "dev"), None),
            P(("grp", "dev"), None),
            P(("grp", "dev"), None),
            P(("grp", "dev"), None, None),
            P("grp", None),
            P("grp", None, "dev"),
            P(("grp", "dev"), None),
        ),
        out_specs=P(("grp", "dev"), None),
        check_vma=False,
    )
```

profile of v0, /device:TPU:24, one launch (start us, length us, event | category | flops | bytes accessed | tf_op | source)
XLA Modules:
  0.0 288.4 jit_solution(11970384998128103651)
XLA Ops:
  10.1 2.1 fusion.64
  13.9 16.5 %all_to_all.15 = f32[32,1,2048]{2,1,0:T(1,128)S(1)} all-to-all(f32[32,1,2048]{2,1,0:T(1,128)S(1)} %copy.29), channel_id=1, replica_groups=mesh['grp'=4,'dev'=32] {'dev'}, dimensions={0} | all-to-all | bytes 524288 | tf_op jit(solution)/shard_map/all_to_all | solution.py:49
  30.7 12.7 %all_to_all.16 = f32[32,1,2048]{2,1,0:T(1,128)S(1)} all-to-all(f32[32,1,2048]{2,1,0:T(1,128)S(1)} %broadcast_in_dim.48), channel_id=1, replica_groups=mesh['grp'=4,'dev'=32] {'dev'}, dimensions={0} | all-to-all | bytes 524288 | tf_op jit(solution)/shard_map/all_to_all | solution.py:25
  45.3 2.6 collective-permute-start.1
  47.9 5.6 %collective-permute-start = (f32[1024,256]{1,0:T(8,128)S(1)}, f32[1024,256]{1,0:T(8,128)}, u32[]{:S(2)}, u32[]{:S(2)}) collective-permute-start(f32[1024,256]{1,0:T(8,128)S(1)} %constant_dynamic-update-slice_fusion), channel_id=1, source_target_pairs={{0,1},{1,2},{2,3},{3,4},{4,5},{5,6},{6,7},{7,8},{8,9},{9,10},{10,1... | collective-permute-start | bytes 3145736 | tf_op jit(solution)/shard_map/ppermute | solution.py:75
  53.5 18.1 %collective-permute-done.1 = f32[1024,256]{1,0:T(8,128)S(1)} collective-permute-done((f32[1024,256]{1,0:T(8,128)S(1)}, f32[1024,256]{1,0:T(8,128)S(1)}, u32[]{:S(2)}, u32[]{:S(2)}) %collective-permute-start.1) | collective-permute-done | bytes 1048608 | tf_op jit(solution)/shard_map/ppermute | solution.py:77
  76.5 43.4 %while.30 = (s32[]{:T(128)}, f32[1,1024,128]{2,1,0:T(8,128)}, s32[3]{0:T(128)S(1)}, f32[3072,128]{1,0:T(8,128)S(1)}, f32[3072,128]{1,0:T(8,128)}, /*index=5*/s32[]{:T(128)}, s32[1]{0:T(128)}) while((s32[]{:T(128)}, f32[1,1024,128]{2,1,0:T(8,128)}, s32[3]{0:T(128)S(1)}, f32[3072,128]{1,0:T(8,128)S(1)}, f32[3072,128]{1,0:T(8,128)}, ...), condition=%wide.region_5.6_spmd.clone, body=%wide.region_0.5_spmd.clone.sunk | while | flops 3226073088 | bytes 13124057 | solution.py:119
  77.7 11.3 %conditional.3 = (f32[1024,128]{1,0:T(8,128)S(1)}) conditional(s32[]{:T(128)} %bitcast.75, () %tuple.91, (s32[]{:T(128)}, s32[3]{0:T(128)S(1)}, f32[3072,128]{1,0:T(8,128)S(1)}, s32[3]{0:T(128)S(1)}, f32[3072,128]{1,0:T(8,128)}, /*index=5*/s32[3]{0:T(128)S(1)}, s32[3]{0:T(128)S(1)}, s32[3]{0:T(128)S(1)}, s32[3]{0:T(128)S(1)}) %tuple.92), branch_computations={%region_1.1_spmd, %region_2.0_spmd.clone} | conditional | flops 3225942016 | bytes 11550970 | solution.py:116
  80.5 3.5 %fusion.41 = f32[1024,1024]{1,0:T(8,128)S(1)} fusion(f32[3072,128]{1,0:T(8,128)S(1)} %get-tuple-element.468, s32[]{:T(128)S(6)} %select_n.86, s32[]{:T(128)S(6)} %select_n.85), kind=kOutput, calls=%fused_computation.49 | convolution fusion | flops 1610612736 | bytes 5242888 | tf_op jit(solution)/shard_map/while/body/eval_jaxpr/cond/branch_1_fun/dot_general | solution.py:87
  84.0 5.0 %fusion.30 = f32[1024,128]{1,0:T(8,128)S(1)} fusion(f32[1024,1024]{1,0:T(8,128)S(1)} %fusion.41, f32[1024]{0:T(1024)S(1)} %get-tuple-element.488, f32[1024]{0:T(1024)S(1)} %get-tuple-element.487, f32[3072,128]{1,0:T(8,128)} %get-tuple-element.471, s32[]{:T(128)S(6)} %select_n.86), kind=kOutput, calls=%fused_computation.36 | convolution fusion | flops 1614807040 | bytes 5251076 | tf_op jit(solution)/shard_map/while/body/eval_jaxpr/cond/branch_1_fun/dot_general | solution.py:106
  89.1 1.9 fusion.100
  92.2 11.3 %conditional.3 = (f32[1024,128]{1,0:T(8,128)S(1)}) conditional(s32[]{:T(128)} %bitcast.75, () %tuple.91, (s32[]{:T(128)}, s32[3]{0:T(128)S(1)}, f32[3072,128]{1,0:T(8,128)S(1)}, s32[3]{0:T(128)S(1)}, f32[3072,128]{1,0:T(8,128)}, /*index=5*/s32[3]{0:T(128)S(1)}, s32[3]{0:T(128)S(1)}, s32[3]{0:T(128)S(1)}, s32[3]{0:T(128)S(1)}) %tuple.92), branch_computations={%region_1.1_spmd, %region_2.0_spmd.clone} | conditional | flops 3225942016 | bytes 11550970 | solution.py:116
  95.0 3.5 %fusion.41 = f32[1024,1024]{1,0:T(8,128)S(1)} fusion(f32[3072,128]{1,0:T(8,128)S(1)} %get-tuple-element.468, s32[]{:T(128)S(6)} %select_n.86, s32[]{:T(128)S(6)} %select_n.85), kind=kOutput, calls=%fused_computation.49 | convolution fusion | flops 1610612736 | bytes 5242888 | tf_op jit(solution)/shard_map/while/body/eval_jaxpr/cond/branch_1_fun/dot_general | solution.py:87
  98.5 5.0 %fusion.30 = f32[1024,128]{1,0:T(8,128)S(1)} fusion(f32[1024,1024]{1,0:T(8,128)S(1)} %fusion.41, f32[1024]{0:T(1024)S(1)} %get-tuple-element.488, f32[1024]{0:T(1024)S(1)} %get-tuple-element.487, f32[3072,128]{1,0:T(8,128)} %get-tuple-element.471, s32[]{:T(128)S(6)} %select_n.86), kind=kOutput, calls=%fused_computation.36 | convolution fusion | flops 1614807040 | bytes 5251076 | tf_op jit(solution)/shard_map/while/body/eval_jaxpr/cond/branch_1_fun/dot_general | solution.py:106
  103.5 1.9 fusion.100
  106.7 11.3 %conditional.3 = (f32[1024,128]{1,0:T(8,128)S(1)}) conditional(s32[]{:T(128)} %bitcast.75, () %tuple.91, (s32[]{:T(128)}, s32[3]{0:T(128)S(1)}, f32[3072,128]{1,0:T(8,128)S(1)}, s32[3]{0:T(128)S(1)}, f32[3072,128]{1,0:T(8,128)}, /*index=5*/s32[3]{0:T(128)S(1)}, s32[3]{0:T(128)S(1)}, s32[3]{0:T(128)S(1)}, s32[3]{0:T(128)S(1)}) %tuple.92), branch_computations={%region_1.1_spmd, %region_2.0_spmd.clone} | conditional | flops 3225942016 | bytes 11550970 | solution.py:116
  109.4 3.5 %fusion.41 = f32[1024,1024]{1,0:T(8,128)S(1)} fusion(f32[3072,128]{1,0:T(8,128)S(1)} %get-tuple-element.468, s32[]{:T(128)S(6)} %select_n.86, s32[]{:T(128)S(6)} %select_n.85), kind=kOutput, calls=%fused_computation.49 | convolution fusion | flops 1610612736 | bytes 5242888 | tf_op jit(solution)/shard_map/while/body/eval_jaxpr/cond/branch_1_fun/dot_general | solution.py:87
  113.0 5.0 %fusion.30 = f32[1024,128]{1,0:T(8,128)S(1)} fusion(f32[1024,1024]{1,0:T(8,128)S(1)} %fusion.41, f32[1024]{0:T(1024)S(1)} %get-tuple-element.488, f32[1024]{0:T(1024)S(1)} %get-tuple-element.487, f32[3072,128]{1,0:T(8,128)} %get-tuple-element.471, s32[]{:T(128)S(6)} %select_n.86), kind=kOutput, calls=%fused_computation.36 | convolution fusion | flops 1614807040 | bytes 5251076 | tf_op jit(solution)/shard_map/while/body/eval_jaxpr/cond/branch_1_fun/dot_general | solution.py:106
  118.0 1.9 fusion.100
  121.1 6.0 %fusion.66 = f32[1024,1024]{1,0:T(8,128)} fusion(f32[1024,128]{1,0:T(8,128)S(1)} %copy-done.1, f32[1024,256]{1,0:T(8,128)} %all-gather.5.cloned.1.call-done), kind=kOutput, calls=%fused_computation.80 | convolution fusion | flops 1610612736 | bytes 5242880 | tf_op jit(solution)/shard_map/dot_general | solution.py:87
  127.2 80.1 %all-gather.3.cloned.1.call-done = f32[4096,256]{0,1:T(8,128)} async-done(((f32[128,256]{0,1:T(8,128)}), f32[4096,256]{0,1:T(8,128)}) %all-gather.3.cloned.1.call-update) | async-done | bytes 4194320 | tf_op jit(solution)/shard_map/all_gather | solution.py:11
  207.3 4.6 %fusion.82 = (f32[4096,128]{0,1:T(8,128)}, f32[4096,128]{0,1:T(8,128)}) fusion(f32[4096,256]{0,1:T(8,128)} %all-gather.3.cloned.1.call-done), kind=kLoop, calls=%fused_computation.109 | loop fusion | bytes 8388608 | tf_op jit(solution)/shard_map/slice | solution.py:13
  211.9 59.2 %while.31 = (s32[]{:T(128)}, f32[1,1024,128]{2,1,0:T(8,128)S(1)}, f32[1024]{0:T(1024)S(1)}, f32[4096,128]{0,1:T(8,128)}, f32[1024,128]{1,0:T(8,128)S(1)}, /*inde...) while((s32[]{:T(128)}, f32[1,1024,128]{2,1,0:T(8,128)S(1)}, ...), condition=%wide.region_10.11_spmd.clone, body=%wide.region_7.10_spmd.clone.sunk | while | flops 1613180928 | bytes 8671461 | solution.py:168
  215.4 3.9 %fusion.107 = f32[1,1024,128]{2,1,0:T(8,128)S(1)} fusion(f32[512,1024]{1,0:T(8,128)S(1)} %fusion.105, f32[512]{0:T(512)S(1)} %multiply_reduce_fusion.6, f32[1024]{0:T(1024)S(1)} %get-tuple-element.656, f32[1,1024,128]{2,1,0:T(8,128)S(1)} %get-tuple-element.643, f32[512,128]{1,0:T(8,128)S(1)} %copy.35, pred[]{:T(512)S(6)} %compare.22, ...), kind=kOutput, calls=%fused_computation.11.clone.1 | convolution fusion | flops 807731200 | bytes 3416065 | tf_op jit(solution)/shard_map/while/body/eval_jaxpr/tpb,tbr->tpr/dot_general | solution.py:166
  222.8 3.9 %fusion.107 = f32[1,1024,128]{2,1,0:T(8,128)S(1)} fusion(f32[512,1024]{1,0:T(8,128)S(1)} %fusion.105, f32[512]{0:T(512)S(1)} %multiply_reduce_fusion.6, f32[1024]{0:T(1024)S(1)} %get-tuple-element.656, f32[1,1024,128]{2,1,0:T(8,128)S(1)} %get-tuple-element.643, f32[512,128]{1,0:T(8,128)S(1)} %copy.35, pred[]{:T(512)S(6)} %compare.22, ...), kind=kOutput, calls=%fused_computation.11.clone.1 | convolution fusion | flops 807731200 | bytes 3416065 | tf_op jit(solution)/shard_map/while/body/eval_jaxpr/tpb,tbr->tpr/dot_general | solution.py:166
  230.2 3.9 %fusion.107 = f32[1,1024,128]{2,1,0:T(8,128)S(1)} fusion(f32[512,1024]{1,0:T(8,128)S(1)} %fusion.105, f32[512]{0:T(512)S(1)} %multiply_reduce_fusion.6, f32[1024]{0:T(1024)S(1)} %get-tuple-element.656, f32[1,1024,128]{2,1,0:T(8,128)S(1)} %get-tuple-element.643, f32[512,128]{1,0:T(8,128)S(1)} %copy.35, pred[]{:T(512)S(6)} %compare.22, ...), kind=kOutput, calls=%fused_computation.11.clone.1 | convolution fusion | flops 807731200 | bytes 3416065 | tf_op jit(solution)/shard_map/while/body/eval_jaxpr/tpb,tbr->tpr/dot_general | solution.py:166
  237.5 3.9 %fusion.107 = f32[1,1024,128]{2,1,0:T(8,128)S(1)} fusion(f32[512,1024]{1,0:T(8,128)S(1)} %fusion.105, f32[512]{0:T(512)S(1)} %multiply_reduce_fusion.6, f32[1024]{0:T(1024)S(1)} %get-tuple-element.656, f32[1,1024,128]{2,1,0:T(8,128)S(1)} %get-tuple-element.643, f32[512,128]{1,0:T(8,128)S(1)} %copy.35, pred[]{:T(512)S(6)} %compare.22, ...), kind=kOutput, calls=%fused_computation.11.clone.1 | convolution fusion | flops 807731200 | bytes 3416065 | tf_op jit(solution)/shard_map/while/body/eval_jaxpr/tpb,tbr->tpr/dot_general | solution.py:166
  244.9 3.9 %fusion.107 = f32[1,1024,128]{2,1,0:T(8,128)S(1)} fusion(f32[512,1024]{1,0:T(8,128)S(1)} %fusion.105, f32[512]{0:T(512)S(1)} %multiply_reduce_fusion.6, f32[1024]{0:T(1024)S(1)} %get-tuple-element.656, f32[1,1024,128]{2,1,0:T(8,128)S(1)} %get-tuple-element.643, f32[512,128]{1,0:T(8,128)S(1)} %copy.35, pred[]{:T(512)S(6)} %compare.22, ...), kind=kOutput, calls=%fused_computation.11.clone.1 | convolution fusion | flops 807731200 | bytes 3416065 | tf_op jit(solution)/shard_map/while/body/eval_jaxpr/tpb,tbr->tpr/dot_general | solution.py:166
  252.3 3.9 %fusion.107 = f32[1,1024,128]{2,1,0:T(8,128)S(1)} fusion(f32[512,1024]{1,0:T(8,128)S(1)} %fusion.105, f32[512]{0:T(512)S(1)} %multiply_reduce_fusion.6, f32[1024]{0:T(1024)S(1)} %get-tuple-element.656, f32[1,1024,128]{2,1,0:T(8,128)S(1)} %get-tuple-element.643, f32[512,128]{1,0:T(8,128)S(1)} %copy.35, pred[]{:T(512)S(6)} %compare.22, ...), kind=kOutput, calls=%fused_computation.11.clone.1 | convolution fusion | flops 807731200 | bytes 3416065 | tf_op jit(solution)/shard_map/while/body/eval_jaxpr/tpb,tbr->tpr/dot_general | solution.py:166
  259.7 3.9 %fusion.107 = f32[1,1024,128]{2,1,0:T(8,128)S(1)} fusion(f32[512,1024]{1,0:T(8,128)S(1)} %fusion.105, f32[512]{0:T(512)S(1)} %multiply_reduce_fusion.6, f32[1024]{0:T(1024)S(1)} %get-tuple-element.656, f32[1,1024,128]{2,1,0:T(8,128)S(1)} %get-tuple-element.643, f32[512,128]{1,0:T(8,128)S(1)} %copy.35, pred[]{:T(512)S(6)} %compare.22, ...), kind=kOutput, calls=%fused_computation.11.clone.1 | convolution fusion | flops 807731200 | bytes 3416065 | tf_op jit(solution)/shard_map/while/body/eval_jaxpr/tpb,tbr->tpr/dot_general | solution.py:166
  267.0 3.9 %fusion.107 = f32[1,1024,128]{2,1,0:T(8,128)S(1)} fusion(f32[512,1024]{1,0:T(8,128)S(1)} %fusion.105, f32[512]{0:T(512)S(1)} %multiply_reduce_fusion.6, f32[1024]{0:T(1024)S(1)} %get-tuple-element.656, f32[1,1024,128]{2,1,0:T(8,128)S(1)} %get-tuple-element.643, f32[512,128]{1,0:T(8,128)S(1)} %copy.35, pred[]{:T(512)S(6)} %compare.22, ...), kind=kOutput, calls=%fused_computation.11.clone.1 | convolution fusion | flops 807731200 | bytes 3416065 | tf_op jit(solution)/shard_map/while/body/eval_jaxpr/tpb,tbr->tpr/dot_general | solution.py:166
  271.2 10.4 %fusion.61 = f32[1024,128]{1,0:T(8,128)} fusion(f32[1024,1024]{1,0:T(8,128)} %fusion.66, f32[1024]{0:T(1024)S(1)} %multiply_reduce_fusion.3, f32[1024]{0:T(1024)S(1)} %get-tuple-element.678, f32[1024,256]{1,0:T(8,128)} %all-gather.5.cloned.1.call-done, f32[1,1024,128]{2,1,0:T(8,128)S(1)} %copy-done.2, f32[1,1024,128]{2,1,0:T(8,128)S(1)} %get-tuple-element.369, ...), kind=kOutput, calls=%fused_computation.73 | convolution fusion | flops 1615200256 | bytes 6303744 | tf_op jit(solution)/shard_map/dot_general | solution.py:174
  (141 shorter events, 47.3 us)
Async XLA Ops:
  6.5 3.6 %copy-start = (f32[1,128,1024]{2,1,0:T(8,128)S(1)}, f32[1,128,1024]{2,1,0:T(8,128)}, u32[]{:S(2)}) copy-start(f32[1,128,1024]{2,1,0:T(8,128)} %param.16) | copy-start | bytes 1572868
  6.5 113.3 %all-gather.5.cloned.1.call-start = ((), (), s32[]{:S(2)}) async-start(), calls=%async_computation.3 | async-start | bytes 1310720 | tf_op jit(solution)/shard_map/all_gather | solution.py:11
  10.1 34.9 %copy-start.1 = (f32[1024,128]{1,0:T(8,128)S(1)}, f32[1024,128]{1,0:T(8,128)}, u32[]{:S(2)}) copy-start(f32[1024,128]{1,0:T(8,128)} %param.13) | copy-start | bytes 1572868
  12.2 33.0 %copy-start.4 = (f32[1024,128]{1,0:T(8,128)S(1)}, f32[1024,128]{1,0:T(8,128)}, u32[]{:S(2)}) copy-start(f32[1024,128]{1,0:T(8,128)} %param.14) | copy-start | bytes 1572868
  13.6 39.9 %copy-start.5 = (s32[1,3]{1,0:T(1,128)S(1)}, s32[1,3]{1,0:T(1,128)}, u32[]{:S(2)}) copy-start(s32[1,3]{1,0:T(1,128)} %param.19) | copy-start | bytes 40
  44.2 163.1 %all-gather.3.cloned.1.call-start = ((), (), s32[]{:S(2)}) async-start(), calls=%async_computation.2 | async-start | bytes 4325376 | tf_op jit(solution)/shard_map/all_gather | solution.py:11
  45.3 26.3 %collective-permute-start.1 = (f32[1024,256]{1,0:T(8,128)S(1)}, f32[1024,256]{1,0:T(8,128)S(1)}, u32[]{:S(2)}, u32[]{:S(2)}) collective-permute-start(f32[1024,256]{1,0:T(8,128)S(1)} %constant_dynamic-update-slice_fusion), channel_id=1, source_target_pairs={{1,0},{2,1},{3,2},{4,3},{5,4},{6,5},{7,6},{8,7},{9,8},{10,9},{11,1... | collective-permute-start | bytes 3145736 | tf_op jit(solution)/shard_map/ppermute | solution.py:77
  47.9 24.9 %collective-permute-start = (f32[1024,256]{1,0:T(8,128)S(1)}, f32[1024,256]{1,0:T(8,128)}, u32[]{:S(2)}, u32[]{:S(2)}) collective-permute-start(f32[1024,256]{1,0:T(8,128)S(1)} %constant_dynamic-update-slice_fusion), channel_id=1, source_target_pairs={{0,1},{1,2},{2,3},{3,4},{4,5},{5,6},{6,7},{7,8},{8,9},{9,10},{10,1... | collective-permute-start | bytes 3145736 | tf_op jit(solution)/shard_map/ppermute | solution.py:75
  127.2 84.8 %copy-start.3 = (f32[1,1024,128]{2,1,0:T(8,128)S(1)}, f32[1,1024,128]{2,1,0:T(8,128)}, u32[]{:S(2)}) copy-start(f32[1,1024,128]{2,1,0:T(8,128)} %custom-call.2) | copy-start | bytes 1572868
  211.9 59.3 %copy-start.2 = (f32[1,1024,128]{2,1,0:T(8,128)S(1)}, f32[1,1024,128]{2,1,0:T(8,128)}, u32[]{:S(2)}) copy-start(f32[1,1024,128]{2,1,0:T(8,128)} %get-tuple-element.368) | copy-start | bytes 1572868
Sparse Core Ops, SparseCore 0:
  44.3 19.7 all-gather.4
  65.6 141.6 all-gather.2
where the time goes:
time: 289 us; the launch traced here: 288 us
  waiting for transfers between devices  99.5 us (34%)
  matrix products  92 us (32%)
  blocking collectives  29.2 us (10%)
  local copies, waits for them, and re-layouts  25.4 us (9%)
  other arithmetic  14 us (5%)
  between operations  13.6 us (5%)
  starting transfers between devices  8.18 us (3%)
  loops' own time  6.47 us (2%)
    all_gather x2, waiting for transfers between devices, in_one_piece(): result, at, done = (lax.all_gather(both, axis, axis=dim, tiled=True), 0, [])  80.1 us
    dot_general x12, matrix products, kernel_tile(): jnp.dot(left, right.T, precision=PRECISION_HIGH, preferred_element_type=j...  31.3 us
    dot_general x8, matrix products, block(): jnp.einsum('tpb,tbr->tpr', tile, far_w, precision=PRECISION_HIGH)  31.1 us
    ppermute x1, waiting for transfers between devices, extended(): lax.ppermute(head, axis, [((i + 1) % count, i) for i in range(ends)])  18.1 us
    all_to_all x1, blocking collectives, sent_and_summed(): lax.all_to_all(blocks, axis, split_axis=0, concat_axis=0, tiled=True)  16.5 us
    dot_general x3, matrix products, compute(): jnp.dot(kernel_tile(target, source), source_w, precision=PRECISION_HIGH,...  15 us
    all_to_all x1, blocking collectives, copy_for_each(): lax.all_to_all(jnp.broadcast_to(shard[None], (size, *shard.shape)), axis,...  12.7 us
    dot_general x1, matrix products, local(): jnp.dot(kernel_tile(points, top_piece_pts), kept, precision=PRECISION_HIG...  10.4 us
  transfers between devices with their start and end apart: 4, of which 3 were waited for; matrix products, arithmetic and copies ran while one was open for 17% of the time, Pallas kernels for 0%

commit v1 on v0

v1 whole, which is shorter than its diff:
```python
import functools
import math

import jax
import jax.numpy as jnp
from jax import lax
from jax.experimental import pallas as pl
from jax.experimental.pallas import tpu as pltpu
from jax.sharding import PartitionSpec as P


LOG2E = math.log2(math.e)
BF = jnp.bfloat16
F32 = jnp.float32
VMEM = pl.BlockSpec(memory_space=pltpu.VMEM)
SMEM = pl.BlockSpec(memory_space=pltpu.SMEM)
NX, NZ, NY = 2, 4, 4
ROWS = 256


def halves(x):
    hi = x.astype(BF)
    return hi, (x - hi.astype(F32)).astype(BF)


def thirds(x):
    hi = x.astype(BF)
    rest = x - hi.astype(F32)
    mid = rest.astype(BF)
    return hi, mid, (rest - mid.astype(F32)).astype(BF)


def dot_nt(a, b):
    return lax.dot_general(a, b, (((1,), (1,)), ((), ())), preferred_element_type=F32)


def dot_nn(a, b):
    return lax.dot_general(a, b, (((1,), (0,)), ((), ())), preferred_element_type=F32)


def dot_tn(a, b):
    return lax.dot_general(a, b, (((0,), (0,)), ((), ())), preferred_element_type=F32)


def dot_full(a, b):
    ah, al = halves(a)
    bh, bl = halves(b)
    return dot_nn(ah, bh) + (dot_nn(ah, bl) + dot_nn(al, bh))


def prep_kernel(skel_ref, near_ref, top_ref, pts_ref, wts_ref, proj_ref, sub_ref, block_ref, mine_ref, other_ref, joined_ref, picked, part, sems):
    feats = pts_ref.shape[1]
    skel = block_ref.shape[0]
    half = mine_ref.shape[0]
    copies = [
        pltpu.make_async_copy(ref, joined_ref.at[:, pl.ds(c * feats, feats)], sems.at[c])
        for c, ref in enumerate((pts_ref, wts_ref))
    ]
    for c in copies:
        c.start()

    def pick(i, carry):
        picked[pl.ds(i, 1), :] = pts_ref[pl.ds(skel_ref[0, i], 1), :]
        return carry

    lax.fori_loop(0, skel, pick, 0, unroll=16)
    block_ref[:, :feats] = picked[...]
    block_ref[:, feats:] = dot_full(proj_ref[0], wts_ref[...])
    pos = lax.axis_index("dev")
    rows = lax.broadcasted_iota(jnp.int32, (skel, top_ref.shape[1]), 0) + pos * skel
    hot = (rows == top_ref[...]).astype(F32).astype(BF)
    hi, mid, lo = thirds(picked[...])
    part[:, :feats] = dot_tn(hot, hi) + (dot_tn(hot, mid) + dot_tn(hot, lo))
    part[:, feats:] = dot_full(sub_ref[0], block_ref[:, feats:])
    x = pos // (NZ * NY)
    mine_ref[...] = part[pl.ds(pl.multiple_of(x * half, half), half), :]
    other_ref[:half, :] = part[pl.ds(pl.multiple_of((1 - x) * half, half), half), :]
    for slot in range(8):
        value = near_ref[0, min(slot, 2)].astype(F32)
        other_ref[half + slot:half + slot + 1, :] = jnp.full((1, 2 * feats), value, F32)
    for c in copies:
        c.wait()


def prepare(near, skel_index, top_index, points, weights, projection, subtree_projection):
    skel = skel_index.shape[1]
    feats = points.shape[1]
    half = top_index.shape[1] // NX
    return pl.pallas_call(
        prep_kernel,
        out_shape=(
            jax.ShapeDtypeStruct((skel, 2 * feats), F32),
            jax.ShapeDtypeStruct((half, 2 * feats), F32),
            jax.ShapeDtypeStruct((half + 8, 2 * feats), F32),
            jax.ShapeDtypeStruct((points.shape[0], 2 * feats), F32),
        ),
        in_specs=[SMEM] * 2 + [VMEM] * 5,
        out_specs=(VMEM, VMEM, VMEM, pl.BlockSpec(memory_space=pl.ANY)),
        scratch_shapes=[pltpu.VMEM((skel, feats), F32), pltpu.VMEM((NX * half, 2 * feats), F32), pltpu.SemaphoreType.DMA((2,))],
        name="prep",
    )(skel_index, near, top_index, points, weights, projection, subtree_projection)


WIDTH = {"pair": 2, "pick": 3}


class Chosen:
    def __init__(self, copies, choice):
        self.copies, self.choice = copies, choice

    def start(self):
        for n, copy in enumerate(self.copies):
            pl.when(self.choice == n)(copy.start)

    def wait(self):
        self.copies[0].wait()


def tiles_kernel(chunks, first, last, across, near_hbm, tgt_hbm, *refs):
    count = sum(WIDTH.get(kind[0], 1) for chunk in chunks for kind, _ in chunk)
    if not first:
        total_hbm, refs = refs[0], refs[1:]
    src_hbm, refs = refs[:count], refs[count:]
    out_ref, near, tgt, cat, total, sems = refs[:6]
    bufs = refs[6:]
    leaf, feats = tgt.shape
    tail = near_hbm.shape[0] - near.shape[0]
    copies = [
        pltpu.make_async_copy(near_hbm.at[pl.ds(tail, 8), pl.ds(0, feats)], near, sems.at[0]),
        pltpu.make_async_copy(tgt_hbm, tgt, sems.at[1]),
    ]
    pos = lax.axis_index("dev")
    waits, i = [], 0
    for chunk, buf in zip(chunks, bufs):
        mine, row = [], 0
        for kind, shape in chunk:
            rows = pl.ds(row, shape[0])
            if kind[0] == "pair":
                for c in range(2):
                    part = buf.at[rows, pl.ds(c * feats, feats)]
                    mine.append(pltpu.make_async_copy(src_hbm[i + c], part, sems.at[2 + i + c]))
                i += 2
            elif kind[0] == "pick":
                if kind[1] == 0:
                    choice = jnp.where(pos == NZ * NY, 2, jnp.where((pos % NY == 0) & (pos > 0), 1, 0))
                else:
                    choice = jnp.where(pos == NZ * NY - 1, 2, jnp.where((pos % NY == NY - 1) & (pos < NX * NZ * NY - 1), 1, 0))
                each = [pltpu.make_async_copy(src_hbm[i + c], buf.at[rows, :], sems.at[2 + i]) for c in range(3)]
                mine.append(Chosen(each, choice))
                i += 3
            else:
                mine.append(pltpu.make_async_copy(src_hbm[i], buf.at[rows, :], sems.at[2 + i]))
                i += 1
            row += shape[0]
        copies += mine
        waits.append(mine)
    if not first:
        copies.append(pltpu.make_async_copy(total_hbm, total, sems.at[2 + count]))
    for c in copies:
        c.start()
    copies[0].wait()
    copies[1].wait()
    hi, lo = halves(tgt[...] * LOG2E)
    cat[:, :feats] = hi
    cat[:, feats:] = lo
    own = (pos + NZ * NY) % (NX * NZ * NY) if across else pos
    x, z, y = pos // (NZ * NY), (pos // NY) % NZ, pos % NY

    def far_keep(k, j):
        leaf_id = device(x, z + (NZ - k), y + (0, 3, 1, 2)[j])
        keep = jnp.ones((1, feats), F32)
        for slot in range(3):
            hit = (leaf_id - own + 1 == slot).astype(F32)
            keep = keep - hit * near[slot:slot + 1, :]
        return keep

    for n, (chunk, buf) in enumerate(zip(chunks, bufs)):
        for c in waits[n]:
            c.wait()
        src = buf[:, :feats]
        parts, row = [], 0
        for kind, shape in chunk:
            if kind[0] == "far":
                each = shape[0] // NY
                for j in range(NY):
                    parts.append(buf[row + j * each:row + (j + 1) * each, feats:] * far_keep(kind[1], j))
            elif kind[0] == "top":
                parts.append(buf[row:row + shape[0], feats:])
            else:
                parts.append(buf[row:row + shape[0], feats:] * near[kind[1]:kind[1] + 1, :])
            row += shape[0]
        wts = parts[0] if len(parts) == 1 else jnp.concatenate(parts, axis=0)
        wts = wts * jnp.exp(-0.5 * jnp.sum(src * src, axis=1, keepdims=True))
        src_hi, src_lo = halves(src)
        src_twice = jnp.concatenate([src_hi, src_hi], axis=1)
        w_cat = jnp.concatenate(halves(wts), axis=1)
        if n == 0 and not first:
            copies[-1].wait()
        for m in range(0, leaf, ROWS):
            at = pl.ds(m, ROWS)
            arg = dot_nt(cat[at, :], src_twice) + dot_nt(cat[at, :feats], src_lo)
            e_hi, e_lo = halves(jnp.exp2(arg))
            both = dot_nn(e_hi, w_cat) + dot_nn(e_lo, w_cat)
            value = both[:, :feats] + both[:, feats:]
            if not (first and n == 0):
                value = value + total[at, :]
            if n < len(chunks) - 1:
                total[at, :] = value
            else:
                if last:
                    here = tgt[at, :]
                    value = value * jnp.exp(-0.5 * jnp.sum(here * here, axis=1, keepdims=True))
                out_ref[at, :] = value


def add_tiles(across, near, targets, chunks, total=None, last=False):
    leaf, feats = targets.shape
    first = total is None
    arrays = [a for chunk in chunks for _, *group in chunk for a in group]
    shapes = [[(kind, group[0].shape) for kind, *group in chunk] for chunk in chunks]
    args = [near, targets] + ([] if first else [total]) + arrays
    sizes = [sum(shape[0] for _, shape in chunk) for chunk in shapes]
    rows = sum(sizes)
    return pl.pallas_call(
        functools.partial(tiles_kernel, shapes, first, last, across),
        out_shape=jax.ShapeDtypeStruct((leaf, feats), F32),
        in_specs=[pl.BlockSpec(memory_space=pl.ANY)] * len(args),
        out_specs=VMEM,
        scratch_shapes=[
            pltpu.VMEM((8, feats), F32),
            pltpu.VMEM((leaf, feats), F32),
            pltpu.VMEM((leaf, 2 * feats), BF),
            pltpu.VMEM((leaf, feats), F32),
            pltpu.SemaphoreType.DMA((len(arrays) + 3,)),
        ]
        + [pltpu.VMEM((size, 2 * feats), F32) for size in sizes],
        compiler_params=pltpu.CompilerParams(vmem_limit_bytes=40 << 20),
        cost_estimate=pl.CostEstimate(
            flops=16 * leaf * rows * feats, transcendentals=leaf * rows, bytes_accessed=8 * (rows + 2 * leaf) * feats
        ),
        name="tiles",
    )(*args)


def place(i):
    return i // (NZ * NY), (i // NY) % NZ, i % NY


def device(x, z, y):
    return (x % NX) * NZ * NY + (z % NZ) * NY + y % NY


def shift(a, dx, dz, dy):
    pairs = []
    for i in range(NX * NZ * NY):
        x, z, y = place(i)
        pairs.append((i, device(x + dx, z + dz, y + dy)))
    return lax.ppermute(a, "dev", pairs)


def swap(a, bz, by):
    pairs = []
    for i in range(NX * NZ * NY):
        x, z, y = place(i)
        pairs.append((i, device(x, z ^ bz, y ^ by)))
    return lax.ppermute(a, "dev", pairs)


def group_swap(a, bit):
    return lax.ppermute(a, "grp", [(i, i ^ bit) for i in range(4)])


def local(points, weights, skel_index, projection, top_index, subtree_projection, near_leaf_mask):
    targets = shift(points, 1, 0, 0)
    block, mine, other, joined = prepare(
        near_leaf_mask, skel_index, top_index, points, weights, projection, subtree_projection
    )
    own_near = other

    ring = (1, 3, 2)
    by_y = [block]
    for k in ring:
        by_y.append(shift(block, 0, 0, k))
    plane = jnp.concatenate(by_y, axis=0)
    by_z = {0: plane}
    for k in ring:
        by_z[k] = shift(plane, 0, k, 0)

    count = lax.axis_size("dev")
    count = lax.axis_size("dev")
    middle = NZ * NY
    inside = [i for i in range(1, count) if i % NY]
    above = [lax.ppermute(joined, "dev", [(i - 1, i) for i in inside])]
    below = [lax.ppermute(joined, "dev", [(i, i - 1) for i in inside])]
    for ends in ([i for i in range(NY, count, NY) if i != middle], [middle]):
        pairs = [(i - 1, i) for i in ends] + [(i, i - 1) for i in ends]
        corner = lax.ppermute(joined, "dev", pairs)
        above.append(corner)
        below.append(corner)

    got = shift(other, 1, 0, 0)
    mine = mine + got[: mine.shape[0]]
    for bz, by in ((1, 0), (3, 0), (0, 1), (0, 3)):
        peer = swap(mine, bz, by)
        mine = mine + peer
    two = group_swap(mine, 1)
    pair_of = jnp.concatenate([mine, two], axis=0)
    four = group_swap(pair_of, 2)

    far = lambda k: (("far", k), by_z[k])
    top = [(("top",), two), (("top",), four)]
    total = add_tiles(False, own_near, points, [[(("pair", 1), points, weights)]])
    side = add_tiles(True, got, targets, [[far(0)]])
    side = add_tiles(True, got, targets, [[far(1), far(3)]], side)
    side = add_tiles(True, got, targets, [[far(2)] + top], side, last=True)
    back = shift(side, 1, 0, 0)
    total = add_tiles(False, own_near, points, [[far(0), far(2)] + top, [far(1), far(3)]], total)
    total = add_tiles(False, own_near, points, [[(("pick", 0), *above)], [(("pick", 2), *below)]], total, last=True)
    return total + back


def solution(mesh):
    return jax.shard_map(
        local,
        mesh=mesh,
        in_specs=(
            P(("grp", "dev"), None),
            P(("grp", "dev"), None),
            P(("grp", "dev"), None),
            P(("grp", "dev"), None, None),
            P("grp", None),
            P("grp", None, "dev"),
            P(("grp", "dev"), None),
        ),
        out_specs=P(("grp", "dev"), None),
        check_vma=False,
    )
```

time: 289 us -> 99.8 us (0.35)
  the two profiles are of different devices: /device:TPU:24 before, /device:TPU:0 now
where the time goes in v1:
time: 99.8 us; the launch traced here: 99.6 us
  starting transfers between devices  52.6 us (53%)
  Pallas kernels  28.7 us (29%)
  waiting for transfers between devices  16 us (16%)
  local copies, waits for them, and re-layouts  1 us (1%)
    ppermute x9, starting transfers between devices, shift(): return lax.ppermute(a, 'dev', pairs)  35.1 us
    pallas_call x6, Pallas kernels, add_tiles(): pl.pallas_call(functools.partial(tiles_kernel, shapes, first, last, acros...  25.5 us
    ppermute x4, waiting for transfers between devices, swap(): return lax.ppermute(a, 'dev', pairs)  9.37 us
    ppermute x4, starting transfers between devices, swap(): return lax.ppermute(a, 'dev', pairs)  8.54 us
    ppermute x9, waiting for transfers between devices, shift(): return lax.ppermute(a, 'dev', pairs)  6.67 us
    ppermute x2, starting transfers between devices, group_swap(): return lax.ppermute(a, 'grp', [(i, i ^ bit) for i in range(4)])  3.37 us
    pallas_call x1, Pallas kernels, prepare(): pl.pallas_call(prep_kernel, out_shape=(jax.ShapeDtypeStruct((skel, 2 * fe...  3.21 us
    ppermute x1, starting transfers between devices, local(): above = [lax.ppermute(joined, 'dev', [(i - 1, i) for i in inside])]  2.9 us
  transfers between devices with their start and end apart: 19, of which 7 were waited for; matrix products, arithmetic and copies ran while one was open for 1% of the time, Pallas kernels for 26%

profile of v1, /device:TPU:0, one launch (start us, length us, event | category | flops | bytes accessed | tf_op | source)
XLA Modules:
  0.0 99.6 jit_solution(12473121361388311480)
XLA Ops:
  0.0 3.2 %prep.1 = (f32[128,256]{1,0:T(8,128)}, f32[128,256]{1,0:T(8,128)}, f32[136,256]{1,0:T(8,128)}, f32[1024,256]{1,0:T(8,128)}) custom-call(s32[1,128]{1,0:T(1,128)} %skel_ref.1, s32[1,3]{1,0:T(1,128)} %near_ref.1, s32[1,256]{1,0:T(1,128)} %top_ref.1, f32[1024,128]{1,0:T(8,128)} %tgt_hbm.5, f32[1024,128]{1,0:T(8,128)} %refs_1_.1, f32[1,128,1024]{2,1,0:T(8,128)} %proj_ref.1, ...), custom_call_target="tpu_custom_call" | custom-call | tf_op jit(solution)/shard_map/prep/pallas_call | solution.py:89
  3.2 1.7 %collective-permute-start.4 = (f32[136,256]{1,0:T(8,128)}, f32[136,256]{1,0:T(8,128)S(1)}, u32[]{:S(2)}, u32[]{:S(2)}) collective-permute-start(f32[136,256]{1,0:T(8,128)} %get-tuple-element.9.near_hbm), channel_id=1, source_target_pairs={{0,16},{1,17},{2,18},{3,19},{4,20},{5,21},{6,22},{7,23},{8,24},{9,... | collective-permute-start | bytes 417800 | tf_op jit(solution)/shard_map/ppermute | solution.py:258
  4.9 0.4 collective-permute-start.17
  5.3 3.3 %collective-permute-start.2 = (f32[128,256]{1,0:T(8,128)}, f32[128,256]{1,0:T(8,128)S(1)}, u32[]{:S(2)}, u32[]{:S(2)}) collective-permute-start(f32[128,256]{1,0:T(8,128)} %get-tuple-element.10), channel_id=1, source_target_pairs={{0,2},{1,3},{2,0},{3,1},{4,6},{5,7},{6,4},{7,5},{8,10},{9,11},{10,... | collective-permute-start | bytes 393224 | tf_op jit(solution)/shard_map/ppermute | solution.py:258
  8.6 1.1 %collective-permute-start.1 = (f32[128,256]{1,0:T(8,128)}, f32[128,256]{1,0:T(8,128)S(1)}, u32[]{:S(2)}, u32[]{:S(2)}) collective-permute-start(f32[128,256]{1,0:T(8,128)} %get-tuple-element.10), channel_id=1, source_target_pairs={{0,3},{1,0},{2,1},{3,2},{4,7},{5,4},{6,5},{7,6},{8,11},{9,8},{10,9... | collective-permute-start | bytes 393224 | tf_op jit(solution)/shard_map/ppermute | solution.py:258
  9.7 1.0 collective-permute-start
  10.7 0.9 constant_dynamic-update-slice_fusion.3
  11.7 2.0 %collective-permute-start.5 = (f32[128,256]{1,0:T(8,128)S(1)}, f32[128,256]{1,0:T(8,128)S(1)}, u32[]{:S(2)}, u32[]{:S(2)}) collective-permute-start(f32[128,256]{1,0:T(8,128)S(1)} %slice_add_fusion), channel_id=1, source_target_pairs={{0,4},{1,5},{2,6},{3,7},{4,0},{5,1},{6,2},{7,3},{8,12},{9,13},{10,... | collective-permute-start | bytes 393224 | tf_op jit(solution)/shard_map/ppermute | solution.py:266
  13.7 2.4 %collective-permute-done = f32[128,256]{1,0:T(8,128)S(1)} collective-permute-done((f32[128,256]{1,0:T(8,128)}, f32[128,256]{1,0:T(8,128)S(1)}, u32[]{:S(2)}, u32[]{:S(2)}) %collective-permute-start) | collective-permute-done | bytes 131104 | tf_op jit(solution)/shard_map/ppermute | solution.py:258
  16.1 0.6 collective-permute-done.5
  16.7 4.1 %collective-permute-start.6 = (f32[128,256]{1,0:T(8,128)S(1)}, f32[128,256]{1,0:T(8,128)S(1)}, u32[]{:S(2)}, u32[]{:S(2)}) collective-permute-start(f32[128,256]{1,0:T(8,128)S(1)} %add.19), channel_id=1, source_target_pairs={{0,12},{1,13},{2,14},{3,15},{4,8},{5,9},{6,10},{7,11},{8,4},{9,5},... | collective-permute-start | bytes 393224 | tf_op jit(solution)/shard_map/ppermute | solution.py:266
  21.0 2.0 %collective-permute-start.11 = (f32[512,256]{1,0:T(8,128)S(1)}, f32[512,256]{1,0:T(8,128)S(1)}, u32[]{:S(2)}, u32[]{:S(2)}) collective-permute-start(f32[512,256]{1,0:T(8,128)S(1)} %constant_dynamic-update-slice_fusion.refs_1_.refs_0_), channel_id=1, source_target_pairs={{0,4},{1,5},{2,6},{3,7},{4,8},{5,9},{6,10},{7,11},{8,12},{9,13},{1... | collective-permute-start | bytes 1572872 | tf_op jit(solution)/shard_map/ppermute | solution.py:258
  23.0 2.2 %collective-permute-done.6 = f32[128,256]{1,0:T(8,128)S(1)} collective-permute-done((f32[128,256]{1,0:T(8,128)S(1)}, f32[128,256]{1,0:T(8,128)S(1)}, u32[]{:S(2)}, u32[]{:S(2)}) %collective-permute-start.6) | collective-permute-done | bytes 131104 | tf_op jit(solution)/shard_map/ppermute | solution.py:266
  25.5 2.3 %collective-permute-start.3 = (f32[512,256]{1,0:T(8,128)S(1)}, f32[512,256]{1,0:T(8,128)S(1)}, u32[]{:S(2)}, u32[]{:S(2)}) collective-permute-start(f32[512,256]{1,0:T(8,128)S(1)} %constant_dynamic-update-slice_fusion.refs_1_.refs_0_), channel_id=1, source_target_pairs={{0,8},{1,9},{2,10},{3,11},{4,12},{5,13},{6,14},{7,15},{8,0},{9,1},... | collective-permute-start | bytes 1572872 | tf_op jit(solution)/shard_map/ppermute | solution.py:258
  27.8 2.4 %collective-permute-done.7 = f32[128,256]{1,0:T(8,128)S(1)} collective-permute-done((f32[128,256]{1,0:T(8,128)S(1)}, f32[128,256]{1,0:T(8,128)S(1)}, u32[]{:S(2)}, u32[]{:S(2)}) %collective-permute-start.7) | collective-permute-done | bytes 131104 | tf_op jit(solution)/shard_map/ppermute | solution.py:266
  30.3 2.1 %collective-permute-start.8 = (f32[128,256]{1,0:T(8,128)S(1)}, f32[128,256]{1,0:T(8,128)S(1)}, u32[]{:S(2)}, u32[]{:S(2)}) collective-permute-start(f32[128,256]{1,0:T(8,128)S(1)} %add.21), channel_id=1, source_target_pairs={{0,3},{1,2},{2,1},{3,0},{4,7},{5,6},{6,5},{7,4},{8,11},{9,10},{10,... | collective-permute-start | bytes 393224 | tf_op jit(solution)/shard_map/ppermute | solution.py:266
  32.4 4.1 %collective-permute-done.8 = f32[128,256]{1,0:T(8,128)S(1)} collective-permute-done((f32[128,256]{1,0:T(8,128)S(1)}, f32[128,256]{1,0:T(8,128)S(1)}, u32[]{:S(2)}, u32[]{:S(2)}) %collective-permute-start.8) | collective-permute-done | bytes 131104 | tf_op jit(solution)/shard_map/ppermute | solution.py:266
  36.7 3.0 %tiles.6.refs_0_ = f32[1024,128]{1,0:T(8,128)S(1)} custom-call(f32[136,256]{1,0:T(8,128)S(1)} %copy-done.2, f32[1024,128]{1,0:T(8,128)S(1)} %copy-done.1, f32[1024,128]{1,0:T(8,128)S(1)} %copy-done.1, f32[1024,128]{1,0:T(8,128)S(1)} %copy-done), custom_call_target="tpu_custom_call" | custom-call | flops 2147483648 | bytes 3145728 | tf_op jit(solution)/shard_map/tiles/pallas_call | solution.py:224
  39.8 1.3 %collective-permute-start.16 = (f32[1024,256]{1,0:T(8,128)S(1)}, f32[1024,256]{1,0:T(8,128)S(1)}, u32[]{:S(2)}, u32[]{:S(2)}) collective-permute-start(f32[1024,256]{1,0:T(8,128)S(1)} %copy-done.4), channel_id=1, source_target_pairs={{1,0},{2,1},{3,2},{5,4},{6,5},{7,6},{9,8},{10,9},{11,10},{13,12},{... | collective-permute-start | bytes 3145736 | tf_op jit(solution)/shard_map/ppermute | solution.py:294
  41.1 2.8 %collective-permute-done.12.refs_6_.refs_2_ = f32[512,256]{1,0:T(8,128)S(1)} collective-permute-done((f32[512,256]{1,0:T(8,128)S(1)}, f32[512,256]{1,0:T(8,128)S(1)}, u32[]{:S(2)}, u32[]{:S(2)}) %collective-permute-start.12) | collective-permute-done | bytes 524320 | tf_op jit(solution)/shard_map/ppermute | solution.py:258
  43.8 0.7 collective-permute-start.15
  44.5 1.5 %collective-permute-done.11.refs_5_.refs_1_ = f32[512,256]{1,0:T(8,128)S(1)} collective-permute-done((f32[512,256]{1,0:T(8,128)S(1)}, f32[512,256]{1,0:T(8,128)S(1)}, u32[]{:S(2)}, u32[]{:S(2)}) %collective-permute-start.11) | collective-permute-done | bytes 524320 | tf_op jit(solution)/shard_map/ppermute | solution.py:258
  46.0 0.7 collective-permute-start.14
  46.7 2.9 %collective-permute-start.13 = (f32[1024,256]{1,0:T(8,128)S(1)}, f32[1024,256]{1,0:T(8,128)S(1)}, u32[]{:S(2)}, u32[]{:S(2)}) collective-permute-start(f32[1024,256]{1,0:T(8,128)S(1)} %copy-done.4), channel_id=1, source_target_pairs={{0,1},{1,2},{2,3},{4,5},{5,6},{6,7},{8,9},{9,10},{10,11},{12,13},{... | collective-permute-start | bytes 3145736 | tf_op jit(solution)/shard_map/ppermute | solution.py:293
  49.7 3.3 %collective-permute-start.10 = (f32[256,256]{1,0:T(8,128)S(1)}, f32[256,256]{1,0:T(8,128)S(1)}, u32[]{:S(2)}, u32[]{:S(2)}) collective-permute-start(f32[256,256]{1,0:T(8,128)S(1)} %pad_maximum_fusion), channel_id=1, source_target_pairs={{0,64},{32,96},{64,0},{96,32},{1,65},{33,97},{65,1},{97,33},{2,66}... | collective-permute-start | bytes 786440 | tf_op jit(solution)/shard_map/ppermute | solution.py:270
  53.0 1.7 %tiles.9.refs_0_ = f32[1024,128]{1,0:T(8,128)S(1)} custom-call(f32[136,256]{1,0:T(8,128)S(1)} %collective-permute-done.4.near_hbm, f32[1024,128]{1,0:T(8,128)S(1)} %collective-permute-done.17.tgt_hbm, f32[512,256]{1,0:T(8,128)S(1)} %constant_dynamic-update-slice_fusion.refs_1_.refs_0_), custom_call_target="tpu_custom_call" | custom-call | flops 1073741824 | bytes 2621440 | tf_op jit(solution)/shard_map/tiles/pallas_call | solution.py:224
  54.7 3.3 %tiles.10.refs_0_ = f32[1024,128]{1,0:T(8,128)S(1)} custom-call(f32[136,256]{1,0:T(8,128)S(1)} %collective-permute-done.4.near_hbm, f32[1024,128]{1,0:T(8,128)S(1)} %collective-permute-done.17.tgt_hbm, f32[1024,128]{1,0:T(8,128)S(1)} %tiles.9.refs_0_, f32[512,256]{1,0:T(8,128)S(1)} %collective-permute-done.11.refs_5_.refs_1_, ...), custom_call_target="tpu_custom_call" | custom-call | flops 2147483648 | bytes 3145728 | tf_op jit(solution)/shard_map/tiles/pallas_call | solution.py:224
  58.0 3.4 %tiles.11 = f32[1024,128]{1,0:T(8,128)S(1)} custom-call(f32[136,256]{1,0:T(8,128)S(1)} %collective-permute-done.4.near_hbm, f32[1024,128]{1,0:T(8,128)S(1)} %collective-permute-done.17.tgt_hbm, f32[1024,128]{1,0:T(8,128)S(1)} %tiles.10.refs_0_, f32[512,256]{1,0:T(8,128)S(1)} %collective-permute-done.3.refs_2_.refs_1_, ...), custom_call_target="tpu_custom_call" | custom-call | flops 1879048192 | bytes 3014656 | tf_op jit(solution)/shard_map/tiles/pallas_call | solution.py:224
  61.5 23.2 %collective-permute-start.18 = (f32[1024,128]{1,0:T(8,128)S(1)}, f32[1024,128]{1,0:T(8,128)S(1)}, u32[]{:S(2)}, u32[]{:S(2)}) collective-permute-start(f32[1024,128]{1,0:T(8,128)S(1)} %tiles.11), channel_id=1, source_target_pairs={{0,16},{1,17},{2,18},{3,19},{4,20},{5,21},{6,22},{7,23},{8,24},{9,... | collective-permute-start | bytes 1572872 | tf_op jit(solution)/shard_map/ppermute | solution.py:258
  84.7 7.8 %tiles.7.refs_0_ = f32[1024,128]{1,0:T(8,128)S(1)} custom-call(f32[136,256]{1,0:T(8,128)S(1)} %copy-done.2, f32[1024,128]{1,0:T(8,128)S(1)} %copy-done.1, f32[1024,128]{1,0:T(8,128)S(1)} %tiles.6.refs_0_, f32[512,256]{1,0:T(8,128)S(1)} %constant_dynamic-update-slice_fusion.refs_1_.refs_0_, f32[512,256]{1,0:T(8,128)S(1)} %collective-permute-done.3.refs_2_.refs_1_, ...), custom_call_target="tpu_custom_call" | custom-call | flops 5100273664 | bytes 4587520 | tf_op jit(solution)/shard_map/tiles/pallas_call | solution.py:224
  92.5 6.2 %tiles.8 = f32[1024,128]{1,0:T(8,128)S(1)} custom-call(f32[136,256]{1,0:T(8,128)S(1)} %copy-done.2, f32[1024,128]{1,0:T(8,128)S(1)} %copy-done.1, f32[1024,128]{1,0:T(8,128)S(1)} %tiles.7.refs_0_, f32[1024,256]{1,0:T(8,128)S(1)} %collective-permute-done.13.refs_1_, f32[1024,256]{1,0:T(8,128)S(1)} %collective-permute-done.14.refs_2_.refs_5_, ...), custom_call_target="tpu_custom_call" | custom-call | flops 4294967296 | bytes 4194304 | tf_op jit(solution)/shard_map/tiles/pallas_call | solution.py:224
  98.7 0.8 add.23
  (34 shorter events, 0.7 us)
Async XLA Ops:
  0.0 4.9 %copy-start.1 = (f32[1024,128]{1,0:T(8,128)S(1)}, f32[1024,128]{1,0:T(8,128)}, u32[]{:S(2)}) copy-start(f32[1024,128]{1,0:T(8,128)} %tgt_hbm.5) | copy-start | bytes 1572868
  3.2 8.4 %collective-permute-start.4 = (f32[136,256]{1,0:T(8,128)}, f32[136,256]{1,0:T(8,128)S(1)}, u32[]{:S(2)}, u32[]{:S(2)}) collective-permute-start(f32[136,256]{1,0:T(8,128)} %get-tuple-element.9.near_hbm), channel_id=1, source_target_pairs={{0,16},{1,17},{2,18},{3,19},{4,20},{5,21},{6,22},{7,23},{8,24},{9,... | collective-permute-start | bytes 417800 | tf_op jit(solution)/shard_map/ppermute | solution.py:258
  4.9 34.8 %collective-permute-start.17 = (f32[1024,128]{1,0:T(8,128)S(1)}, f32[1024,128]{1,0:T(8,128)S(1)}, u32[]{:S(2)}, u32[]{:S(2)}) collective-permute-start(f32[1024,128]{1,0:T(8,128)S(1)} %copy-done.1), channel_id=1, source_target_pairs={{0,16},{1,17},{2,18},{3,19},{4,20},{5,21},{6,22},{7,23},{8,24},{9,... | collective-permute-start | bytes 1572872 | tf_op jit(solution)/shard_map/ppermute | solution.py:258
  5.3 6.3 %copy-start.3 = (f32[128,256]{1,0:T(8,128)S(1)}, f32[128,256]{1,0:T(8,128)}, u32[]{:S(2)}) copy-start(f32[128,256]{1,0:T(8,128)} %get-tuple-element.11) | copy-start | bytes 393220
  5.3 15.5 %collective-permute-start.2 = (f32[128,256]{1,0:T(8,128)}, f32[128,256]{1,0:T(8,128)S(1)}, u32[]{:S(2)}, u32[]{:S(2)}) collective-permute-start(f32[128,256]{1,0:T(8,128)} %get-tuple-element.10), channel_id=1, source_target_pairs={{0,2},{1,3},{2,0},{3,1},{4,6},{5,7},{6,4},{7,5},{8,10},{9,11},{10,... | collective-permute-start | bytes 393224 | tf_op jit(solution)/shard_map/ppermute | solution.py:258
  8.6 7.5 %collective-permute-start.1 = (f32[128,256]{1,0:T(8,128)}, f32[128,256]{1,0:T(8,128)S(1)}, u32[]{:S(2)}, u32[]{:S(2)}) collective-permute-start(f32[128,256]{1,0:T(8,128)} %get-tuple-element.10), channel_id=1, source_target_pairs={{0,3},{1,0},{2,1},{3,2},{4,7},{5,4},{6,5},{7,6},{8,11},{9,8},{10,9... | collective-permute-start | bytes 393224 | tf_op jit(solution)/shard_map/ppermute | solution.py:258
  9.7 6.4 %collective-permute-start = (f32[128,256]{1,0:T(8,128)}, f32[128,256]{1,0:T(8,128)S(1)}, u32[]{:S(2)}, u32[]{:S(2)}) collective-permute-start(f32[128,256]{1,0:T(8,128)} %get-tuple-element.10), channel_id=1, source_target_pairs={{0,1},{1,2},{2,3},{3,0},{4,5},{5,6},{6,7},{7,4},{8,9},{9,10},{10,1... | collective-permute-start | bytes 393224 | tf_op jit(solution)/shard_map/ppermute | solution.py:258
  11.7 5.0 %collective-permute-start.5 = (f32[128,256]{1,0:T(8,128)S(1)}, f32[128,256]{1,0:T(8,128)S(1)}, u32[]{:S(2)}, u32[]{:S(2)}) collective-permute-start(f32[128,256]{1,0:T(8,128)S(1)} %slice_add_fusion), channel_id=1, source_target_pairs={{0,4},{1,5},{2,6},{3,7},{4,0},{5,1},{6,2},{7,3},{8,12},{9,13},{10,... | collective-permute-start | bytes 393224 | tf_op jit(solution)/shard_map/ppermute | solution.py:266
  16.7 8.5 %collective-permute-start.6 = (f32[128,256]{1,0:T(8,128)S(1)}, f32[128,256]{1,0:T(8,128)S(1)}, u32[]{:S(2)}, u32[]{:S(2)}) collective-permute-start(f32[128,256]{1,0:T(8,128)S(1)} %add.19), channel_id=1, source_target_pairs={{0,12},{1,13},{2,14},{3,15},{4,8},{5,9},{6,10},{7,11},{8,4},{9,5},... | collective-permute-start | bytes 393224 | tf_op jit(solution)/shard_map/ppermute | solution.py:266
  20.9 15.8 %copy-start = (f32[1024,128]{1,0:T(8,128)S(1)}, f32[1024,128]{1,0:T(8,128)}, u32[]{:S(2)}) copy-start(f32[1024,128]{1,0:T(8,128)} %refs_1_.1) | copy-start | bytes 1572868
  20.9 22.9 %collective-permute-start.12 = (f32[512,256]{1,0:T(8,128)S(1)}, f32[512,256]{1,0:T(8,128)S(1)}, u32[]{:S(2)}, u32[]{:S(2)}) collective-permute-start(f32[512,256]{1,0:T(8,128)S(1)} %constant_dynamic-update-slice_fusion.refs_1_.refs_0_), channel_id=1, source_target_pairs={{0,12},{1,13},{2,14},{3,15},{4,0},{5,1},{6,2},{7,3},{8,4},{9,5},{1... | collective-permute-start | bytes 1572872 | tf_op jit(solution)/shard_map/ppermute | solution.py:258
  21.0 25.0 %collective-permute-start.11 = (f32[512,256]{1,0:T(8,128)S(1)}, f32[512,256]{1,0:T(8,128)S(1)}, u32[]{:S(2)}, u32[]{:S(2)}) collective-permute-start(f32[512,256]{1,0:T(8,128)S(1)} %constant_dynamic-update-slice_fusion.refs_1_.refs_0_), channel_id=1, source_target_pairs={{0,4},{1,5},{2,6},{3,7},{4,8},{5,9},{6,10},{7,11},{8,12},{9,13},{1... | collective-permute-start | bytes 1572872 | tf_op jit(solution)/shard_map/ppermute | solution.py:258
  25.2 5.0 %collective-permute-start.7 = (f32[128,256]{1,0:T(8,128)S(1)}, f32[128,256]{1,0:T(8,128)S(1)}, u32[]{:S(2)}, u32[]{:S(2)}) collective-permute-start(f32[128,256]{1,0:T(8,128)S(1)} %add.20), channel_id=1, source_target_pairs={{0,1},{1,0},{2,3},{3,2},{4,5},{5,4},{6,7},{7,6},{8,9},{9,8},{10,11... | collective-permute-start | bytes 393224 | tf_op jit(solution)/shard_map/ppermute | solution.py:266
  25.5 24.2 %collective-permute-start.3 = (f32[512,256]{1,0:T(8,128)S(1)}, f32[512,256]{1,0:T(8,128)S(1)}, u32[]{:S(2)}, u32[]{:S(2)}) collective-permute-start(f32[512,256]{1,0:T(8,128)S(1)} %constant_dynamic-update-slice_fusion.refs_1_.refs_0_), channel_id=1, source_target_pairs={{0,8},{1,9},{2,10},{3,11},{4,12},{5,13},{6,14},{7,15},{8,0},{9,1},... | collective-permute-start | bytes 1572872 | tf_op jit(solution)/shard_map/ppermute | solution.py:258
  30.3 6.4 %copy-start.2 = (f32[136,256]{1,0:T(8,128)S(1)}, f32[136,256]{1,0:T(8,128)}, u32[]{:S(2)}) copy-start(f32[136,256]{1,0:T(8,128)} %get-tuple-element.9.near_hbm) | copy-start | bytes 417796
  30.3 6.3 %collective-permute-start.8 = (f32[128,256]{1,0:T(8,128)S(1)}, f32[128,256]{1,0:T(8,128)S(1)}, u32[]{:S(2)}, u32[]{:S(2)}) collective-permute-start(f32[128,256]{1,0:T(8,128)S(1)} %add.21), channel_id=1, source_target_pairs={{0,3},{1,2},{2,1},{3,0},{4,7},{5,6},{6,5},{7,4},{8,11},{9,10},{10,... | collective-permute-start | bytes 393224 | tf_op jit(solution)/shard_map/ppermute | solution.py:266
  36.6 3.2 %copy-start.4 = (f32[1024,256]{1,0:T(8,128)S(1)}, f32[1024,256]{1,0:T(8,128)}, u32[]{:S(2)}) copy-start(f32[1024,256]{1,0:T(8,128)} %get-tuple-element.12) | copy-start | bytes 3145732
  36.6 10.2 %collective-permute-start.9 = (f32[128,256]{1,0:T(8,128)S(1)}, f32[128,256]{1,0:T(8,128)S(1)}, u32[]{:S(2)}, u32[]{:S(2)}) collective-permute-start(f32[128,256]{1,0:T(8,128)S(1)} %add.22), channel_id=1, source_target_pairs={{0,32},{32,0},{64,96},{96,64},{1,33},{33,1},{65,97},{97,65},{2,34}... | collective-permute-start | bytes 393224 | tf_op jit(solution)/shard_map/ppermute | solution.py:270
  39.8 52.7 %collective-permute-start.16 = (f32[1024,256]{1,0:T(8,128)S(1)}, f32[1024,256]{1,0:T(8,128)S(1)}, u32[]{:S(2)}, u32[]{:S(2)}) collective-permute-start(f32[1024,256]{1,0:T(8,128)S(1)} %copy-done.4), channel_id=1, source_target_pairs={{1,0},{2,1},{3,2},{5,4},{6,5},{7,6},{9,8},{10,9},{11,10},{13,12},{... | collective-permute-start | bytes 3145736 | tf_op jit(solution)/shard_map/ppermute | solution.py:294
  43.8 48.7 %collective-permute-start.15 = (f32[1024,256]{1,0:T(8,128)S(1)}, f32[1024,256]{1,0:T(8,128)S(1)}, u32[]{:S(2)}, u32[]{:S(2)}) collective-permute-start(f32[1024,256]{1,0:T(8,128)S(1)} %copy-done.4), channel_id=1, source_target_pairs={{15,16},{16,15},{47,48},{48,47},{79,80},{80,79},{111,112},{112,111}} | collective-permute-start | bytes 3145736 | tf_op jit(solution)/shard_map/ppermute | solution.py:297
  46.0 46.5 %collective-permute-start.14 = (f32[1024,256]{1,0:T(8,128)S(1)}, f32[1024,256]{1,0:T(8,128)S(1)}, u32[]{:S(2)}, u32[]{:S(2)}) collective-permute-start(f32[1024,256]{1,0:T(8,128)S(1)} %copy-done.4), channel_id=1, source_target_pairs={{3,4},{7,8},{11,12},{19,20},{23,24},{27,28},{4,3},{8,7},{12,11},{2... | collective-permute-start | bytes 3145736 | tf_op jit(solution)/shard_map/ppermute | solution.py:297
  46.7 45.8 %collective-permute-start.13 = (f32[1024,256]{1,0:T(8,128)S(1)}, f32[1024,256]{1,0:T(8,128)S(1)}, u32[]{:S(2)}, u32[]{:S(2)}) collective-permute-start(f32[1024,256]{1,0:T(8,128)S(1)} %copy-done.4), channel_id=1, source_target_pairs={{0,1},{1,2},{2,3},{4,5},{5,6},{6,7},{8,9},{9,10},{10,11},{12,13},{... | collective-permute-start | bytes 3145736 | tf_op jit(solution)/shard_map/ppermute | solution.py:293
  49.7 8.3 %collective-permute-start.10 = (f32[256,256]{1,0:T(8,128)S(1)}, f32[256,256]{1,0:T(8,128)S(1)}, u32[]{:S(2)}, u32[]{:S(2)}) collective-permute-start(f32[256,256]{1,0:T(8,128)S(1)} %pad_maximum_fusion), channel_id=1, source_target_pairs={{0,64},{32,96},{64,0},{96,32},{1,65},{33,97},{65,1},{97,33},{2,66}... | collective-permute-start | bytes 786440 | tf_op jit(solution)/shard_map/ppermute | solution.py:270
  61.5 37.2 %collective-permute-start.18 = (f32[1024,128]{1,0:T(8,128)S(1)}, f32[1024,128]{1,0:T(8,128)S(1)}, u32[]{:S(2)}, u32[]{:S(2)}) collective-permute-start(f32[1024,128]{1,0:T(8,128)S(1)} %tiles.11), channel_id=1, source_target_pairs={{0,16},{1,17},{2,18},{3,19},{4,20},{5,21},{6,22},{7,23},{8,24},{9,... | collective-permute-start | bytes 1572872 | tf_op jit(solution)/shard_map/ppermute | solution.py:258
